TPU v7x, 32 devices: a whole 2x2x4 slice. The times are simulated.
32 devices in a mesh: blk: 8 (over z, x), road: 4 (over y, core).
Axes of the slice: x: 2, y: 2, z: 4, core: 2. Of those that a mesh axis runs over, the one named last changes fastest.
Arguments:
- disp: float32 [3, 16, 64, 1024], P(None, None, 'road', 'blk'), may hold values from -1.2 to 1.2
- veloc: float32 [3, 16, 64, 1024], P(None, None, 'road', 'blk'), may hold values from -6 to 6
- stiff: float32 [3, 16, 64, 1024], P(None, None, 'road', 'blk'), may hold values from 0.5 to 2
- mass: float32 [16, 64, 1024], P(None, 'road', 'blk'), may hold values from 1 to 4
- road_height: float32 [16384], P('road'), may hold values from -1.2 to 1.2
- road_slope_x: float32 [16384], P('road'), may hold values from -0.3 to 0.3
- road_slope_y: float32 [16384], P('road'), may hold values from -0.3 to 0.3
- road_stiff: float32 [16384], P('road'), may hold values from 1 to 4
- tile_list: int32 [8, 4, 4], P('blk', 'road'), may hold values from 0 to 63, as said below
- pair_node: int32 [8, 4, 8192], P('blk', 'road'), may hold values from 0 to 2047, as said below
- pair_slot: int32 [8, 4, 8192], P('blk', 'road'), may hold values from 0 to 1023, as said below
- pair_count: int32 [8, 4], P('blk', 'road'), may hold values from 0 to 8192, as said below
Outputs:
- veloc_out: float32 [3, 16, 64, 1024], P(None, None, 'road', 'blk')
- road_load: float32 [16384], P(('blk', 'road'))
Inputs may be any that keep to these rules, and one draw needn't show every extreme that they name: `pair_count`: the sectors with live slots form one run of 1 consecutive sectors round the cycle, possibly across its end; on their devices from 4096 to 8192 slots are live, and some device has all 8192 live; on all other devices none. Index of a node of the device's own outer layer: lateral position pair_node // 128, circumferential position pair_node % 128 within the device's block. Position within the device's listed tiles: tile pair_slot // 256, facet pair_slot % 256 of that tile. `tile_list`: 4 consecutive tile numbers counted modulo 64; tile t holds facets t * 256 to t * 256 + 255, on road patch t // 16.
All inputs are finite; a program needn't handle non-finite values.
Results may differ from a plain program's by a relative error of at most 0.0001.
Values sent between devices are 32-bit elements; how exact they have to be, the bound alone decides.
A program may use at most 64 MiB of HBM per device.

v0:
```python
import jax
import jax.numpy as jnp
from jax import lax
from jax.sharding import PartitionSpec as P

PAIR_BLOCK = 1024
TILE = 256
TILES_NEED = 4
STEPS = 2


hardening = 0.5
time_step = 0.25


def with_halo(block, sides, width, periodic):
    for axis, dim in sides:
        count = lax.axis_size(axis)
        forward = [(i, i + 1) for i in range(count - 1)]
        if periodic:
            forward.append((count - 1, 0))
        backward = [(target, source) for source, target in forward]
        low = lax.ppermute(
            lax.slice_in_dim(block, block.shape[dim] - width, None, axis=dim), axis, forward
        )
        high = lax.ppermute(lax.slice_in_dim(block, 0, width, axis=dim), axis, backward)
        block = jnp.concatenate([low, block, high], axis=dim)
    return block


def shifted(block, axis, distance):
    devices = range(lax.axis_size(axis))
    route = [((i - distance) % len(devices), i) for i in devices]
    return lax.ppermute(block, axis, route)


def stress_term(strain):
    squared = jnp.sum(strain * strain, axis=0, keepdims=True)
    return strain * (1.0 + hardening * squared)


def edge_force(padded, stiff_padded, which_dim):
    length = padded.shape[which_dim]
    strain = lax.slice_in_dim(padded, 1, length, axis=which_dim) - lax.slice_in_dim(
        padded, 0, length - 1, axis=which_dim
    )
    weights = lax.slice_in_dim(stiff_padded, 1, length, axis=which_dim - 1)
    tension = weights[None] * stress_term(strain)
    return lax.slice_in_dim(tension, 1, length - 1, axis=which_dim) - lax.slice_in_dim(
        tension, 0, length - 2, axis=which_dim
    )


def internal_force(displace, stiffness):
    radial = jnp.pad(displace, ((0, 0), (1, 1), (0, 0), (0, 0)))
    radial_stiff = jnp.pad(stiffness[0], ((1, 1), (0, 0), (0, 0)))
    summed = edge_force(radial, radial_stiff, 1)
    band_rim = with_halo(
        jnp.concatenate([displace, stiffness[1:2]], axis=0), (("road", 2),), 1, False
    )
    summed = summed + edge_force(band_rim[:3], band_rim[3], 2)
    cycle_rim = with_halo(
        jnp.concatenate([displace, stiffness[2:3]], axis=0), (("blk", 3),), 1, True
    )
    return summed + edge_force(cycle_rim[:3], cycle_rim[3], 3)


def press(values):
    return values[6] * jnp.maximum(
        values[3] + values[4] * values[0] + values[5] * values[1] - values[2], 0.0
    )


def gather_pairs(outer_layer, facets, tile_ids, node_ids, slot_ids):
    within = slot_ids // TILE
    tile_pick = jnp.zeros_like(slot_ids)
    for entry_index in range(TILES_NEED):
        tile_pick = tile_pick + jnp.where(within == entry_index, tile_ids[entry_index], 0)
    facet_ids = tile_pick * TILE + slot_ids % TILE
    picked = outer_layer[:, node_ids]
    looked = jnp.stack(
        [facets[0][facet_ids], facets[1][facet_ids], facets[2][facet_ids], facets[3][facet_ids]]
    )
    return (jnp.concatenate([picked, looked], axis=0), facet_ids)


def deposit(force_acc, load_acc, node_ids, values, facet_ids, normal_force):
    contact = jnp.stack([-values[4] * normal_force, -values[5] * normal_force, normal_force])
    return (force_acc.at[:, node_ids].add(contact), load_acc.at[facet_ids].add(normal_force))


def run_blocks(
    outer_layer, facets, tile_ids, node_ids, slot_ids, live_count, outer_force, facet_load
):

    def run_one_block(block_index, carry):
        force_acc, load_acc = carry
        first_slot = block_index * PAIR_BLOCK
        block_nodes = lax.dynamic_slice_in_dim(node_ids, first_slot, PAIR_BLOCK)
        block_slots = lax.dynamic_slice_in_dim(slot_ids, first_slot, PAIR_BLOCK)
        values, facet_ids = gather_pairs(outer_layer, facets, tile_ids, block_nodes, block_slots)
        live_slots = first_slot + jnp.arange(PAIR_BLOCK, dtype=jnp.int32) < live_count
        normal_force = jnp.where(live_slots, press(values), 0.0)
        return deposit(force_acc, load_acc, block_nodes, values, facet_ids, normal_force)

    blocks = (live_count + PAIR_BLOCK - 1) // PAIR_BLOCK
    return lax.fori_loop(0, blocks, run_one_block, (outer_force, facet_load))


def partner_press(received, received_count):

    def partner_one_block(block_index, pressed):
        first_slot = block_index * PAIR_BLOCK
        values = lax.dynamic_slice_in_dim(received, first_slot, PAIR_BLOCK, axis=1)
        live_slots = first_slot + jnp.arange(PAIR_BLOCK, dtype=jnp.int32) < received_count
        normal_force = jnp.where(live_slots, press(values), 0.0)
        return lax.dynamic_update_slice_in_dim(pressed, normal_force, first_slot, axis=0)

    blocks = (received_count + PAIR_BLOCK - 1) // PAIR_BLOCK
    return lax.fori_loop(0, blocks, partner_one_block, jnp.zeros((received.shape[1],), jnp.float32))


def on_device(
    disp,
    veloc,
    stiff,
    mass,
    road_height,
    road_slope_x,
    road_slope_y,
    road_stiff,
    tile_list,
    pair_node,
    pair_slot,
    pair_count,
):
    facets = (
        lax.all_gather(road_height, "road", axis=0, tiled=True),
        lax.all_gather(road_slope_x, "road", axis=0, tiled=True),
        lax.all_gather(road_slope_y, "road", axis=0, tiled=True),
        lax.all_gather(road_stiff, "road", axis=0, tiled=True),
    )
    tile_ids = tile_list[0, 0]
    node_ids = pair_node[0, 0]
    slot_ids = pair_slot[0, 0]
    live_count = pair_count[0, 0]
    half_pairs = node_ids.shape[0] // 2
    half_cycle = lax.axis_size("blk") // 2
    displace = disp
    velocity = veloc
    facet_load = jnp.zeros(facets[0].shape, jnp.float32)
    for step_index in range(STEPS):
        outer_layer = displace[:, -1].reshape(3, -1)
        outer_force = jnp.zeros_like(outer_layer)
        near_count = jnp.minimum(live_count, half_pairs)
        outer_force, facet_load = run_blocks(
            outer_layer,
            facets,
            tile_ids,
            node_ids[:half_pairs],
            slot_ids[:half_pairs],
            near_count,
            outer_force,
            facet_load,
        )
        far_values, far_ids = gather_pairs(
            outer_layer, facets, tile_ids, node_ids[half_pairs:], slot_ids[half_pairs:]
        )
        far_count = jnp.maximum(live_count - half_pairs, 0).reshape(1)
        received, received_count = shifted((far_values, far_count), "blk", half_cycle)
        pressed = partner_press(received, received_count[0])
        returned = shifted(pressed, "blk", half_cycle)
        outer_force, facet_load = deposit(
            outer_force, facet_load, node_ids[half_pairs:], far_values, far_ids, returned
        )
        forces = internal_force(displace, stiff)
        forces = forces.at[:, -1].add(outer_force.reshape(3, displace.shape[2], displace.shape[3]))
        velocity = velocity + time_step * forces / mass[None]
        displace = displace + time_step * velocity
    own_block = lax.psum_scatter(facet_load, ("blk", "road"), scatter_dimension=0, tiled=True)
    return (velocity, own_block)


def solution(mesh):
    in_specs = (
        P(None, None, "road", "blk"),
        P(None, None, "road", "blk"),
        P(None, None, "road", "blk"),
        P(None, "road", "blk"),
        P("road"),
        P("road"),
        P("road"),
        P("road"),
        P("blk", "road", None),
        P("blk", "road", None),
        P("blk", "road", None),
        P("blk", "road"),
    )
    out_specs = (P(None, None, "road", "blk"), P(("blk", "road")))
    return jax.shard_map(
        on_device, mesh=mesh, in_specs=in_specs, out_specs=out_specs, check_vma=False
    )
```

profile of v0, /device:TPU:0, one launch (start us, length us, event | category | flops | bytes accessed | tf_op | source)
XLA Modules:
  0.0 837.7 jit_solution(16092691105079951329)
XLA Ops:
  7.3 1.1 slice_bitcast_fusion
  8.4 2.3 pad_maximum_fusion.9
  10.7 3.0 collective-permute-start.2
  13.7 3.1 collective-permute-start.3
  17.5 1.4 collective-permute-start
  18.9 1.3 collective-permute-start.1
  20.9 7.4 collective-permute-start.4
  28.4 5.2 all_gather.12
  33.7 5.2 all_gather.13
  38.9 5.2 all_gather.14
  44.1 1.4 copy.80
  45.5 5.2 all_gather.15
  52.4 3.5 compare_select_fusion.6
  56.5 23.0 %gather_fusion.12 = f32[4096]{0:T(1024)S(1)} fusion(f32[16384]{0:T(1024)S(1)} %get-tuple-element.1041, s32[4096]{0:T(1024)S(1)} %broadcast_clamp_fusion.5), kind=kCustom, calls=%fused_computation.12 | custom fusion | bytes 49152 | tf_op jit(solution)/shard_map/gather | solution.py:82
  79.6 23.0 %gather_fusion.10 = f32[4096]{0:T(1024)S(1)} fusion(f32[16384]{0:T(1024)S(1)} %get-tuple-element.1039, s32[4096]{0:T(1024)S(1)} %broadcast_clamp_fusion.5), kind=kCustom, calls=%fused_computation.10 | custom fusion | bytes 49152 | tf_op jit(solution)/shard_map/gather | solution.py:82
  102.6 23.0 %gather_fusion.13 = f32[4096]{0:T(1024)S(1)} fusion(f32[16384]{0:T(1024)S(1)} %get-tuple-element.1042, s32[4096]{0:T(1024)S(1)} %broadcast_clamp_fusion.5), kind=kCustom, calls=%fused_computation.13 | custom fusion | bytes 49152 | tf_op jit(solution)/shard_map/gather | solution.py:82
  125.7 23.0 %gather_fusion.14 = f32[4096]{0:T(1024)S(1)} fusion(f32[16384]{0:T(1024)S(1)} %get-tuple-element.1040, s32[4096]{0:T(1024)S(1)} %broadcast_clamp_fusion.5), kind=kCustom, calls=%fused_computation.14 | custom fusion | bytes 49152 | tf_op jit(solution)/shard_map/gather | solution.py:82
  148.7 15.4 %gather_fusion.11 = f32[4096,3]{1,0:T(8,128)} fusion(f32[3,2048]{0,1:T(8,128)} %get-tuple-element.1043, s32[4096]{0:T(1024)S(1)} %broadcast_clamp_fusion.4), kind=kCustom, calls=%fused_computation.11 | custom fusion | bytes 114688 | tf_op jit(solution)/shard_map/gather | solution.py:80
  164.1 2.2 copy.81
  168.5 1.3 multiply_reduce_fusion.1
  169.9 1.1 fusion.34
  171.1 2.2 multiply_multiply_fusion.1
  173.5 1.0 multiply_multiply_fusion.3
  174.5 2.3 collective-permute-start.6
  176.7 1.8 fusion.30
  179.2 2.0 copy.82
  181.2 23.1 %scatter_fusion.4 = f32[3,2048]{0,1:T(8,128)S(1)} fusion(f32[3,2048]{0,1:T(8,128)S(1)} %get-tuple-element.418, s32[4096]{0:T(1024)S(1)} %bitcast.180, f32[4096,3]{1,0:T(8,128)} %copy.82), kind=kCustom, calls=%fused_computation.20 | custom fusion | flops 12288 | bytes 163840 | tf_op jit(solution)/shard_map/scatter-add | solution.py:89
  204.8 1.1 pad_maximum_fusion.8
  206.0 0.9 collective-permute-start.9
  206.9 3.8 collective-permute-start.10
  211.5 1.3 collective-permute-start.7
  212.7 1.3 collective-permute-start.8
  214.1 1.4 copy.84
  215.4 23.8 %scatter_fusion.5 = f32[16384]{0:T(1024)S(1)} fusion(f32[16384]{0:T(1024)S(1)} %get-tuple-element.420, s32[4096]{0:T(1024)S(1)} %bitcast.177, f32[4096]{0:T(1024)S(1)} %copy-done.29), kind=kCustom, calls=%fused_computation.21 | custom fusion | flops 4096 | bytes 65536 | tf_op jit(solution)/shard_map/scatter-add | solution.py:89
  239.4 0.9 copy-done.8
  240.4 16.7 %gather_fusion.15 = f32[4096,3]{1,0:T(8,128)} fusion(f32[3,2048]{0,1:T(8,128)} %get-tuple-element.1083, s32[4096]{0:T(1024)} %copy-done.30), kind=kCustom, calls=%fused_computation.15 | custom fusion | bytes 114688 | tf_op jit(solution)/shard_map/gather | solution.py:80
  257.1 2.2 copy.85
  260.5 146.7 %collective-permute-done.10 = f32[4,16,16,1]{3,2,1,0:T(8,128)} collective-permute-done((f32[4,16,16,1]{3,2,1,0:T(8,128)}, f32[4,16,16,1]{3,2,1,0:T(8,128)}, u32[]{:S(2)}, u32[]{:S(2)}) %collective-permute-start.10) | collective-permute-done | bytes 4128 | tf_op jit(solution)/shard_map/ppermute | solution.py:26
  407.2 1.3 multiply_reduce_fusion
  408.5 1.1 fusion.37
  409.8 2.2 multiply_multiply_fusion
  413.0 2.8 collective-permute-start.12
  415.8 1.5 fusion.28
  417.7 2.0 copy.86
  419.7 23.1 %scatter_fusion.6 = f32[3,2048]{0,1:T(8,128)S(1)} fusion(f32[3,2048]{0,1:T(8,128)S(1)} %get-tuple-element.1073, s32[4096]{0:T(1024)S(1)} %bitcast.181, f32[4096,3]{1,0:T(8,128)} %copy.86), kind=kCustom, calls=%fused_computation.22 | custom fusion | flops 12288 | bytes 163840 | tf_op jit(solution)/shard_map/scatter-add | solution.py:89
  443.1 23.8 %scatter_fusion.7 = f32[16384]{0:T(1024)S(1)} fusion(f32[16384]{0:T(1024)S(1)} %get-tuple-element.1074, s32[4096]{0:T(1024)S(1)} %bitcast.178, f32[4096]{0:T(1024)S(1)} %collective-permute-done.12), kind=kCustom, calls=%fused_computation.23 | custom fusion | flops 4096 | bytes 65536 | tf_op jit(solution)/shard_map/scatter-add | solution.py:89
  468.5 361.0 %all-reduce.6.cloned.1.call-done = f32[16384]{0:T(1024)} async-done(((f32[16384]{0:T(1024)}), f32[16384]{0:T(1024)}) %all-reduce.6.cloned.1.call-update) | async-done | bytes 65552
  829.5 1.3 dynamic-slice.14
  (140 shorter events, 11.5 us)
Async XLA Ops:
  7.2 9.6 %copy-start.1 = (f32[3,16,16,128]{3,2,1,0:T(8,128)S(1)}, f32[3,16,16,128]{3,2,1,0:T(8,128)}, u32[]{:S(2)}) copy-start(f32[3,16,16,128]{3,2,1,0:T(8,128)} %param.24) | copy-start | bytes 1179652
  7.2 36.9 %slice-start = ((f32[3,16,16,128]{3,2,1,0:T(8,128)}), f32[3,1,16,128]{3,2,1,0:T(8,128)S(1)}, s32[]{:S(2)}) async-start(f32[3,16,16,128]{3,2,1,0:T(8,128)} %param.24), calls=%async_computation.1 | async-start | bytes 49152 | tf_op jit(solution)/shard_map/slice | solution.py:153
  7.2 21.2 %copy-start.18 = (s32[1,1,8192]{2,1,0:T(1,128)S(1)}, s32[1,1,8192]{2,1,0:T(1,128)}, u32[]{:S(2)}) copy-start(s32[1,1,8192]{2,1,0:T(1,128)} %param.33) | copy-start | bytes 98308
  7.2 21.2 %copy-start.36 = (f32[4096]{0:T(1024)S(1)}, f32[4096]{0:T(1024)}, u32[]{:S(2)}) copy-start(f32[4096]{0:T(1024)} %param.29) | copy-start | bytes 49156
  7.2 26.5 %copy-start.37 = (f32[4096]{0:T(1024)S(1)}, f32[4096]{0:T(1024)}, u32[]{:S(2)}) copy-start(f32[4096]{0:T(1024)} %param.31) | copy-start | bytes 49156
  7.2 31.7 %copy-start.38 = (f32[4096]{0:T(1024)S(1)}, f32[4096]{0:T(1024)}, u32[]{:S(2)}) copy-start(f32[4096]{0:T(1024)} %param.28) | copy-start | bytes 49156
  7.2 822.3 %all-reduce.6.cloned.1.call-start = ((), (), s32[]{:S(2)}) async-start(), calls=%async_computation | async-start | bytes 131072
  8.4 37.1 %copy-start.39 = (f32[4096]{0:T(1024)S(1)}, f32[4096]{0:T(1024)}, u32[]{:S(2)}) copy-start(f32[4096]{0:T(1024)} %param.30) | copy-start | bytes 49156
  8.4 42.3 %copy-start.9 = (s32[1,1,4]{2,1,0:T(1,128)S(1)}, s32[1,1,4]{2,1,0:T(1,128)}, u32[]{:S(2)}) copy-start(s32[1,1,4]{2,1,0:T(1,128)} %param.32) | copy-start | bytes 52
  10.7 40.7 %slice-start.1 = ((s32[1,1,8192]{2,1,0:T(1,128)}), s32[1,1,4096]{2,1,0:T(1,128)S(1)}, s32[]{:S(2)}) async-start(s32[1,1,8192]{2,1,0:T(1,128)} %param.33), calls=%async_computation.2 | async-start | bytes 32768 | tf_op jit(solution)/shard_map/slice | solution.py:160
  10.7 40.7 %slice-start.2 = ((s32[1,1,8192]{2,1,0:T(1,128)}), s32[1,1,4096]{2,1,0:T(1,128)S(1)}, s32[]{:S(2)}) async-start(s32[1,1,8192]{2,1,0:T(1,128)} %param.34), calls=%async_computation.3 | async-start | bytes 32768 | tf_op jit(solution)/shard_map/slice | solution.py:161
  10.7 157.8 %collective-permute-start.2 = (f32[4,16,16,1]{3,2,1,0:T(8,128)}, f32[4,16,16,1]{3,2,1,0:T(8,128)S(1)}, u32[]{:S(2)}, u32[]{:S(2)}) collective-permute-start(f32[4,16,16,1]{3,2,1,0:T(8,128)} %get-tuple-element.551), channel_id=1, source_target_pairs={{0,4},{4,8},{8,12},{12,16},{16,20},{20,24},{24,28},{28,0},{1,5},{5... | collective-permute-start | bytes 12296 | tf_op jit(solution)/shard_map/ppermute | solution.py:23
  13.7 154.8 %collective-permute-start.3 = (f32[4,16,16,1]{3,2,1,0:T(8,128)}, f32[4,16,16,1]{3,2,1,0:T(8,128)}, u32[]{:S(2)}, u32[]{:S(2)}) collective-permute-start(f32[4,16,16,1]{3,2,1,0:T(8,128)} %get-tuple-element.550), channel_id=1, source_target_pairs={{4,0},{8,4},{12,8},{16,12},{20,16},{24,20},{28,24},{0,28},{5,1},{9... | collective-permute-start | bytes 12296 | tf_op jit(solution)/shard_map/ppermute | solution.py:26
  17.5 155.8 %collective-permute-start = (f32[4,16,1,128]{3,2,1,0:T(1,128)}, f32[4,16,1,128]{3,2,1,0:T(1,128)S(1)}, u32[]{:S(2)}, u32[]{:S(2)}) collective-permute-start(f32[4,16,1,128]{3,2,1,0:T(1,128)} %get-tuple-element.557), channel_id=1, source_target_pairs={{0,1},{1,2},{2,3},{4,5},{5,6},{6,7},{8,9},{9,10},{10,11},{12,13},{... | collective-permute-start | bytes 98312 | tf_op jit(solution)/shard_map/ppermute | solution.py:23
  18.9 154.3 %collective-permute-start.1 = (f32[4,16,1,128]{3,2,1,0:T(1,128)}, f32[4,16,1,128]{3,2,1,0:T(1,128)S(1)}, u32[]{:S(2)}, u32[]{:S(2)}) collective-permute-start(f32[4,16,1,128]{3,2,1,0:T(1,128)} %get-tuple-element.528), channel_id=1, source_target_pairs={{1,0},{2,1},{3,2},{5,4},{6,5},{7,6},{9,8},{10,9},{11,10},{13,12},{... | collective-permute-start | bytes 98312 | tf_op jit(solution)/shard_map/ppermute | solution.py:26
  20.9 146.2 %collective-permute-start.4 = (s32[1]{0:T(128)}, s32[1]{0:T(128)}, u32[]{:S(2)}, u32[]{:S(2)}) collective-permute-start(s32[1]{0:T(128)} %bitcast.44), channel_id=1, source_target_pairs={{16,0},{20,4},{24,8},{28,12},{0,16},{4,20},{8,24},{12,28},{17,1},{... | collective-permute-start | bytes 20 | tf_op jit(solution)/shard_map/ppermute | solution.py:34
  28.4 23.1 %copy-start.15 = (s32[4096,1]{0,1:T(1,128)}, s32[4096,1]{0,1:T(1,128)S(1)}, u32[]{:S(2)}) copy-start(s32[4096,1]{0,1:T(1,128)S(1)} %compare_select_fusion.7) | copy-start | bytes 49156
  51.5 28.0 %copy-start.19 = (s32[4096]{0:T(1024)}, s32[4096]{0:T(1024)S(1)}, u32[]{:S(2)}) copy-start(s32[4096]{0:T(1024)S(1)} %get-tuple-element.1052) | copy-start | bytes 49156
  51.5 28.0 %copy-start.24 = (s32[4096]{0:T(1024)}, s32[4096]{0:T(1024)S(1)}, u32[]{:S(2)}) copy-start(s32[4096]{0:T(1024)S(1)} %get-tuple-element.1071) | copy-start | bytes 49156
  51.5 97.2 %copy-start.30 = (s32[4096]{0:T(1024)}, s32[4096]{0:T(1024)S(1)}, u32[]{:S(2)}) copy-start(s32[4096]{0:T(1024)S(1)} %broadcast_clamp_fusion.4) | copy-start | bytes 49156
  51.6 28.0 %copy-start.7 = (f32[17,16,128]{2,1,0:T(8,128)}, f32[17,16,128]{2,1,0:T(8,128)S(1)}, u32[]{:S(2)}) copy-start(f32[17,16,128]{2,1,0:T(8,128)S(1)} %get-tuple-element.566) | copy-start | bytes 417796
  79.6 86.8 %copy-start.31 = (f32[4096]{0:T(1024)}, f32[4096]{0:T(1024)S(1)}, u32[]{:S(2)}) copy-start(f32[4096]{0:T(1024)S(1)} %gather_fusion.12) | copy-start | bytes 49156
  148.7 19.8 %copy-start.33 = (f32[4096]{0:T(1024)}, f32[4096]{0:T(1024)S(1)}, u32[]{:S(2)}) copy-start(f32[4096]{0:T(1024)S(1)} %gather_fusion.14) | copy-start | bytes 49156
  167.1 7.3 collective-permute-start.5
  174.4 6.8 copy-start.16
  174.5 4.7 collective-permute-start.6
  179.2 25.5 %copy-start.28 = (f32[4096]{0:T(1024)}, f32[4096]{0:T(1024)S(1)}, u32[]{:S(2)}) copy-start(f32[4096]{0:T(1024)S(1)} %collective-permute-done.6) | copy-start | bytes 49156
  179.2 25.4 %copy-start.5 = (f32[3,16,16,128]{3,2,1,0:T(8,128)S(1)}, f32[3,16,16,128]{3,2,1,0:T(8,128)}, u32[]{:S(2)}) copy-start(f32[3,16,16,128]{3,2,1,0:T(8,128)} %param.25) | copy-start | bytes 1179652
  179.2 25.4 %copy-start.10 = (f32[16,16,128]{2,1,0:T(8,128)S(1)}, f32[16,16,128]{2,1,0:T(8,128)}, u32[]{:S(2)}) copy-start(f32[16,16,128]{2,1,0:T(8,128)} %param.27) | copy-start | bytes 393220
  204.6 6.1 copy-start.35
  204.7 6.8 copy-start.2
  204.8 10.6 %copy-start.13 = (s32[4096,1]{0,1:T(1,128)S(1)}, s32[4096,1]{0,1:T(1,128)}, u32[]{:S(2)}) copy-start(s32[4096,1]{0,1:T(1,128)} %copy-done.12) | copy-start | bytes 49156
  204.8 10.6 %copy-start.29 = (f32[4096]{0:T(1024)S(1)}, f32[4096]{0:T(1024)}, u32[]{:S(2)}) copy-start(f32[4096]{0:T(1024)} %copy-done.28) | copy-start | bytes 49156
  206.0 54.5 %collective-permute-start.9 = (f32[4,16,16,1]{3,2,1,0:T(8,128)}, f32[4,16,16,1]{3,2,1,0:T(8,128)S(1)}, u32[]{:S(2)}, u32[]{:S(2)}) collective-permute-start(f32[4,16,16,1]{3,2,1,0:T(8,128)} %get-tuple-element.549), channel_id=1, source_target_pairs={{0,4},{4,8},{8,12},{12,16},{16,20},{20,24},{24,28},{28,0},{1,5},{5... | collective-permute-start | bytes 12296 | tf_op jit(solution)/shard_map/ppermute | solution.py:23
  206.9 200.3 %collective-permute-start.10 = (f32[4,16,16,1]{3,2,1,0:T(8,128)}, f32[4,16,16,1]{3,2,1,0:T(8,128)}, u32[]{:S(2)}, u32[]{:S(2)}) collective-permute-start(f32[4,16,16,1]{3,2,1,0:T(8,128)} %get-tuple-element.548), channel_id=1, source_target_pairs={{4,0},{8,4},{12,8},{16,12},{20,16},{24,20},{28,24},{0,28},{5,1},{9... | collective-permute-start | bytes 12296 | tf_op jit(solution)/shard_map/ppermute | solution.py:26
  211.5 200.5 %collective-permute-start.7 = (f32[4,16,1,128]{3,2,1,0:T(1,128)}, f32[4,16,1,128]{3,2,1,0:T(1,128)S(1)}, u32[]{:S(2)}, u32[]{:S(2)}) collective-permute-start(f32[4,16,1,128]{3,2,1,0:T(1,128)} %get-tuple-element.553), channel_id=1, source_target_pairs={{0,1},{1,2},{2,3},{4,5},{5,6},{6,7},{8,9},{9,10},{10,11},{12,13},{... | collective-permute-start | bytes 98312 | tf_op jit(solution)/shard_map/ppermute | solution.py:23
  212.7 199.2 %collective-permute-start.8 = (f32[4,16,1,128]{3,2,1,0:T(1,128)}, f32[4,16,1,128]{3,2,1,0:T(1,128)S(1)}, u32[]{:S(2)}, u32[]{:S(2)}) collective-permute-start(f32[4,16,1,128]{3,2,1,0:T(1,128)} %get-tuple-element.552), channel_id=1, source_target_pairs={{1,0},{2,1},{3,2},{5,4},{6,5},{7,6},{9,8},{10,9},{11,10},{13,12},{... | collective-permute-start | bytes 98312 | tf_op jit(solution)/shard_map/ppermute | solution.py:26
  215.4 23.9 %copy-start.20 = (s32[4096]{0:T(1024)S(1)}, s32[4096]{0:T(1024)}, u32[]{:S(2)}) copy-start(s32[4096]{0:T(1024)} %copy-done.19) | copy-start | bytes 49156
  215.4 23.9 %copy-start.25 = (s32[4096]{0:T(1024)S(1)}, s32[4096]{0:T(1024)}, u32[]{:S(2)}) copy-start(s32[4096]{0:T(1024)} %copy-done.24) | copy-start | bytes 49156
  240.3 19.0 %copy-start.32 = (f32[4096]{0:T(1024)S(1)}, f32[4096]{0:T(1024)}, u32[]{:S(2)}) copy-start(f32[4096]{0:T(1024)} %copy-done.31) | copy-start | bytes 49156
  240.3 19.0 %copy-start.34 = (f32[4096]{0:T(1024)S(1)}, f32[4096]{0:T(1024)}, u32[]{:S(2)}) copy-start(f32[4096]{0:T(1024)} %copy-done.33) | copy-start | bytes 49156
  260.1 152.2 %collective-permute-start.11 = (f32[7,4096]{1,0:T(8,128)}, f32[7,4096]{1,0:T(8,128)S(1)}, u32[]{:S(2)}, u32[]{:S(2)}) collective-permute-start(f32[7,4096]{1,0:T(8,128)} %concatenate.75), channel_id=1, source_target_pairs={{16,0},{20,4},{24,8},{28,12},{0,16},{4,20},{8,24},{12,28},{17,1},{... | collective-permute-start | bytes 344072 | tf_op jit(solution)/shard_map/ppermute | solution.py:34
  413.0 6.7 copy-start.17
  413.0 4.6 collective-permute-start.12
  417.7 25.4 %copy-start.14 = (s32[4096,1]{0,1:T(1,128)S(1)}, s32[4096,1]{0,1:T(1,128)}, u32[]{:S(2)}) copy-start(s32[4096,1]{0,1:T(1,128)} %copy-done.12) | copy-start | bytes 49156
  443.1 24.5 %copy-start.3 = (f32[3,16,16,128]{3,2,1,0:T(8,128)S(1)}, f32[3,16,16,128]{3,2,1,0:T(8,128)}, u32[]{:S(2)}) copy-start(f32[3,16,16,128]{3,2,1,0:T(8,128)} %copy-done.2) | copy-start | bytes 1179652
  443.1 24.5 %copy-start.6 = (f32[3,16,16,128]{3,2,1,0:T(8,128)S(1)}, f32[3,16,16,128]{3,2,1,0:T(8,128)}, u32[]{:S(2)}) copy-start(f32[3,16,16,128]{3,2,1,0:T(8,128)} %param.25) | copy-start | bytes 1179652
  443.1 24.5 %copy-start.11 = (f32[16,16,128]{2,1,0:T(8,128)S(1)}, f32[16,16,128]{2,1,0:T(8,128)}, u32[]{:S(2)}) copy-start(f32[16,16,128]{2,1,0:T(8,128)} %param.27) | copy-start | bytes 393220
  (5 other events, 6.1 us)
Sparse Core Ops, SparseCore 0:
  467.7 361.7 all-reduce.5
where the time goes:
time: 839 us; the launch traced here: 838 us
  waiting for transfers between devices  509 us (61%)
  local copies, waits for them, and re-layouts  144 us (17%)
  other arithmetic  118 us (14%)
  starting transfers between devices  29.8 us (4%)
  blocking collectives  20.9 us (2%)
  between operations  16.2 us (2%)
    unnamed x2, waiting for transfers between devices  361 us
    ppermute x4, waiting for transfers between devices, with_halo(): lax.ppermute(lax.slice_in_dim(block, 0, width, axis=dim), axis, backward)  147 us
    scatter-add x2, other arithmetic, deposit(): load_acc.at[facet_ids].add(normal_force)  47.7 us
    scatter-add x2, other arithmetic, deposit(): force_acc.at[:, node_ids].add(contact)  46.1 us
    gather x4, local copies, waits for them, and re-layouts, gather_pairs(): picked = outer_layer[:, node_ids]  36.5 us
    gather x1, local copies, waits for them, and re-layouts, gather_pairs(): facets[1][facet_ids]  23 us
    gather x1, local copies, waits for them, and re-layouts, gather_pairs(): facets[2][facet_ids]  23 us
    gather x1, local copies, waits for them, and re-layouts, gather_pairs(): facets[3][facet_ids]  23 us
  transfers between devices with their start and end apart: 14, of which 4 were waited for; matrix products, arithmetic and copies ran while one was open for 21% of the time, Pallas kernels for 0%

commit v1 on v0

v1 whole, which is shorter than its diff:
```python
import functools

import jax
import jax.numpy as jnp
from jax import lax
from jax.experimental import pallas as pl
from jax.experimental.pallas import tpu as pltpu
from jax.sharding import PartitionSpec as P

TILE = 256
LANES = 128
GROUP = 1024

hardening = 0.5
time_step = 0.25

MESH = pl.DeviceIdType.MESH
NT = (((1,), (1,)), ((), ()))


def split_two(x):
    high = x.astype(jnp.bfloat16).astype(jnp.float32)
    return high, x - high


def tension(weights, strain):
    squared = strain[0] * strain[0] + strain[1] * strain[1] + strain[2] * strain[2]
    scaled = weights * (1.0 + hardening * squared)
    return [scaled * s for s in strain]


def kernel(
    n_blk,
    n_road,
    lat,
    in_kernel_sum,
    disp,
    veloc,
    stiff,
    mass,
    height,
    slope_x,
    slope_y,
    road_stiff,
    tiles,
    nodes,
    slots,
    count,
    v_out,
    load_out,
    u1,
    v1,
    force,
    node_hot,
    facet_hot,
    facet_vals,
    facet_all,
    table,
    up_send,
    down_send,
    up_recv,
    down_recv,
    side_up_send,
    side_down_send,
    side_up_recv,
    side_down_recv,
    halo_sems,
    facet_sems,
    *reduction,
):
    b = lax.axis_index("blk")
    r = lax.axis_index("road")
    rows = disp.shape[1]
    layers = rows // lat
    groups = nodes.shape[1] // GROUP
    n_rows = table.shape[1]
    half = table.shape[1] // tiles.shape[1]
    patch_rows = height.shape[0]

    def road_peer(offset):
        return {"blk": b, "road": lax.rem(r + offset, n_road)}

    def blk_peer(offset):
        return {"blk": lax.rem(b + offset, n_blk), "road": r}

    blk_offsets = range(1, n_blk) if in_kernel_sum else sorted({1, n_blk - 1})
    barrier = pltpu.get_barrier_semaphore()
    for offset in blk_offsets:
        pl.semaphore_signal(barrier, inc=1, device_id=blk_peer(offset), device_id_type=MESH)
    for offset in range(1, n_road):
        pl.semaphore_signal(barrier, inc=1, device_id=road_peer(offset), device_id_type=MESH)

    def fill_faces(step, source):
        for c in range(3):
            turned = source[c].T
            up_send[step, c : c + 1, :] = turned[LANES - 1 : LANES, :]
            down_send[step, c : c + 1, :] = turned[0:1, :]
            side_up_send[step, c] = source[c, pl.ds(lat - 1, layers, stride=lat), :]
            side_down_send[step, c] = source[c, pl.ds(0, layers, stride=lat), :]
        if step == 0:
            down_send[step, 3:4, :] = stiff[2].T[0:1, :]
            side_down_send[step, 3] = stiff[1, pl.ds(0, layers, stride=lat), :]

    def halo_copies(step):
        plan = (
            (up_send, up_recv, blk_peer(1)),
            (down_send, down_recv, blk_peer(n_blk - 1)),
            (side_up_send, side_up_recv, road_peer(1)),
            (side_down_send, side_down_recv, road_peer(n_road - 1)),
        )
        return [
            pltpu.make_async_remote_copy(
                src_ref=src.at[step],
                dst_ref=dst.at[step],
                send_sem=halo_sems.at[step, 0, i],
                recv_sem=halo_sems.at[step, 1, i],
                device_id=peer,
                device_id_type=MESH,
            )
            for i, (src, dst, peer) in enumerate(plan)
        ]

    fill_faces(0, disp)

    def make_hot(g, _):
        at = pl.ds(pl.multiple_of(g * GROUP, GROUP), GROUP)
        lane = lax.broadcasted_iota(jnp.int32, (LANES, GROUP), 0)
        node_lane = nodes[:, at] & (LANES - 1)
        slot_lane = slots[:, at] & (LANES - 1)
        node_hot[g] = jnp.where(lane == node_lane, 1.0, 0.0).astype(jnp.bfloat16)
        facet_hot[g] = jnp.where(lane == slot_lane, 1.0, 0.0).astype(jnp.bfloat16)
        return 0

    lax.fori_loop(0, groups, make_hot, 0)

    pl.semaphore_wait(barrier, len(blk_offsets) + n_road - 1)
    halos0 = halo_copies(0)
    for copy in halos0:
        copy.start()
    own = (height, slope_x, slope_y, road_stiff)
    facet_copies = []
    for offset in range(1, n_road):
        for a in range(4):
            copy = pltpu.make_async_remote_copy(
                src_ref=own[a],
                dst_ref=facet_all.at[a * n_road + r],
                send_sem=facet_sems.at[0, a, offset - 1],
                recv_sem=facet_sems.at[1, a, offset - 1],
                device_id=road_peer(offset),
                device_id_type=MESH,
            )
            copy.start()
            facet_copies.append(copy)
    for a in range(4):
        facet_all[a * n_road + r] = own[a][...]

    lat_index = lax.broadcasted_iota(jnp.int32, (lat, LANES), 0)
    lane_index = lax.broadcasted_iota(jnp.int32, (lat, LANES), 1)

    def layer_rows(k):
        return pl.ds(pl.multiple_of(k * lat, lat), lat)

    def inside(source, k, above, rim):
        at = layer_rows(k)
        u = [source[c, at, :] for c in range(3)]
        if rim:
            strain = u
        else:
            below = layer_rows(k - 1)
            strain = [u[c] - source[c, below, :] for c in range(3)]
        radial = tension(stiff[0, at, :], strain)
        side = tension(stiff[1, at, :], [x - pltpu.roll(x, 1, 0) for x in u])
        around = tension(stiff[2, at, :], [x - pltpu.roll(x, 1, 1) for x in u])
        for c in range(3):
            t = jnp.where(lat_index == 0, 0.0, side[c])
            w = jnp.where(lane_index == 0, 0.0, around[c])
            force[c, at, :] = (
                (above[c] - radial[c])
                + (pltpu.roll(t, lat - 1, 0) - t)
                + (pltpu.roll(w, LANES - 1, 1) - w)
            )
        return radial

    def interior(source):
        nothing = tuple(jnp.zeros((lat, LANES), jnp.float32) for _ in range(3))

        def body(i, above):
            return tuple(inside(source, layers - 1 - i, above, False))

        above = lax.fori_loop(0, layers - 1, body, nothing)
        inside(source, 0, above, True)

    def rim_force(step):
        stiff_around = down_recv[0, 3:4, :]
        own_around = down_send[0, 3:4, :]
        low = tension(own_around, [down_send[step, c : c + 1, :] - up_recv[step, c : c + 1, :] for c in range(3)])
        high = tension(stiff_around, [down_recv[step, c : c + 1, :] - up_send[step, c : c + 1, :] for c in range(3)])
        place = lax.broadcasted_iota(jnp.int32, (LANES, rows), 0)
        for c in range(3):
            turned = jnp.where(place == 0, -low[c], jnp.where(place == LANES - 1, high[c], 0.0))
            force[c] = force[c] + turned.T
        first = jnp.where(r == 0, 0.0, 1.0)
        last = jnp.where(r == n_road - 1, 0.0, 1.0)
        low = tension(
            side_down_send[0, 3], [side_down_send[step, c] - first * side_up_recv[step, c] for c in range(3)]
        )
        high = tension(
            last * side_down_recv[0, 3], [side_down_recv[step, c] - side_up_send[step, c] for c in range(3)]
        )
        for c in range(3):
            at = pl.ds(0, layers, stride=lat)
            force[c, at, :] = force[c, at, :] - low[c]
            at = pl.ds(lat - 1, layers, stride=lat)
            force[c, at, :] = force[c, at, :] + high[c]

    live_count = count[0, 0]

    def contact(source):
        outer = [source[c, rows - lat : rows, :] for c in range(3)]
        parts = [split_two(x) for x in outer]
        picked_from = jnp.concatenate([p[0] for p in parts] + [p[1] for p in parts], axis=0).astype(jnp.bfloat16)
        node_row = lax.broadcasted_iota(jnp.int32, (lat, GROUP), 0)
        facet_row = lax.broadcasted_iota(jnp.int32, (n_rows, GROUP), 0)
        slot_lane = lax.broadcasted_iota(jnp.int32, (1, GROUP), 1)

        def body(g, carry):
            pushed, loads = carry
            at = pl.ds(pl.multiple_of(g * GROUP, GROUP), GROUP)
            on_node = node_row == (nodes[:, at] >> 7)
            on_facet = facet_row == (slots[:, at] >> 7)
            found = jnp.dot(picked_from, node_hot[g], preferred_element_type=jnp.float32)
            u = []
            for c in range(3):
                both = found[c * lat : (c + 1) * lat] + found[(3 + c) * lat : (4 + c) * lat]
                u.append(jnp.sum(jnp.where(on_node, both, 0.0), axis=0, keepdims=True))
            values = facet_vals[g]
            h, sx, sy, ks = (values[a : a + 1, :] for a in range(4))
            live = slot_lane + g * GROUP < live_count
            normal = jnp.where(live, ks * jnp.maximum(h + sx * u[0] + sy * u[1] - u[2], 0.0), 0.0)
            high, low = zip(*[split_two(x) for x in (-sx * normal, -sy * normal, normal)])
            spread = jnp.concatenate([jnp.where(on_node, x, 0.0) for x in high + low], axis=0)
            pushed = pushed + lax.dot_general(
                spread.astype(jnp.bfloat16), node_hot[g], NT, preferred_element_type=jnp.float32
            )
            heaped = jnp.concatenate([jnp.where(on_facet, x, 0.0) for x in (high[2], low[2])], axis=0)
            loads = loads + lax.dot_general(
                heaped.astype(jnp.bfloat16), facet_hot[g], NT, preferred_element_type=jnp.float32
            )
            return pushed, loads

        pushed, loads = lax.fori_loop(
            0,
            groups,
            body,
            (jnp.zeros((6 * lat, LANES), jnp.float32), jnp.zeros((2 * n_rows, LANES), jnp.float32)),
        )
        outer_force = [pushed[c * lat : (c + 1) * lat] + pushed[(3 + c) * lat : (4 + c) * lat] for c in range(3)]
        return outer_force, loads[:n_rows] + loads[n_rows:]

    def add_outer(outer_force):
        for c in range(3):
            force[c, rows - lat : rows, :] = force[c, rows - lat : rows, :] + outer_force[c]

    interior(disp)

    for copy in facet_copies:
        copy.wait()
    for j in range(tiles.shape[1]):
        for i in range(half):
            row = tiles[0, j] * half + i
            for a in range(4):
                table[a, j * half + i : j * half + i + 1, :] = facet_all[
                    a * n_road + row // patch_rows, pl.ds(row % patch_rows, 1), :
                ]
    parts = [split_two(table[a]) for a in range(4)]
    looked_from = jnp.concatenate([p[0] for p in parts] + [p[1] for p in parts], axis=0).astype(jnp.bfloat16)

    def look_up(g, _):
        at = pl.ds(pl.multiple_of(g * GROUP, GROUP), GROUP)
        on_facet = lax.broadcasted_iota(jnp.int32, (n_rows, GROUP), 0) == (slots[:, at] >> 7)
        found = jnp.dot(looked_from, facet_hot[g], preferred_element_type=jnp.float32)
        for a in range(4):
            both = found[a * n_rows : (a + 1) * n_rows] + found[(4 + a) * n_rows : (5 + a) * n_rows]
            facet_vals[g, a : a + 1, :] = jnp.sum(jnp.where(on_facet, both, 0.0), axis=0, keepdims=True)
        return 0

    lax.fori_loop(0, groups, look_up, 0)
    outer_force, loads0 = contact(disp)
    add_outer(outer_force)

    for copy in halos0:
        copy.wait()
    rim_force(0)

    def advance(k, _):
        at = layer_rows(k)
        scale = time_step / mass[at, :]
        for c in range(3):
            v = veloc[c, at, :] + scale * force[c, at, :]
            v1[c, at, :] = v
            u1[c, at, :] = disp[c, at, :] + time_step * v
        return 0

    lax.fori_loop(0, layers, advance, 0)
    fill_faces(1, u1)
    halos1 = halo_copies(1)
    for copy in halos1:
        copy.start()

    outer_force, loads1 = contact(u1)
    loads = loads0 + loads1

    def dense(shape, row_of):
        row = row_of(shape)
        total = jnp.zeros(shape, jnp.float32)
        for j in range(n_rows):
            here = tiles[0, j // half] * half + j % half
            line = loads[j : j + 1, :].reshape((1,) * (len(shape) - 1) + (LANES,))
            total = total + jnp.where(row == here, line, 0.0)
        return total

    if in_kernel_sum:
        spread_out, road_recv, reduced, blk_recv, road_sems, blk_sems = reduction
        chunk_rows = load_out.shape[0]
        for to in range(n_road):
            spread_out[to] = dense(
                (n_blk, chunk_rows, LANES),
                lambda s: (lax.broadcasted_iota(jnp.int32, s, 0) * n_road + to) * chunk_rows
                + lax.broadcasted_iota(jnp.int32, s, 1),
            )
        road_copies = []
        for offset in range(1, n_road):
            copy = pltpu.make_async_remote_copy(
                src_ref=spread_out.at[lax.rem(r + offset, n_road)],
                dst_ref=road_recv.at[offset - 1],
                send_sem=road_sems.at[0, offset - 1],
                recv_sem=road_sems.at[1, offset - 1],
                device_id=road_peer(offset),
                device_id_type=MESH,
            )
            copy.start()
            road_copies.append(copy)
    else:
        load_out[...] = dense(load_out.shape, lambda s: lax.broadcasted_iota(jnp.int32, s, 0))

    interior(u1)
    add_outer(outer_force)

    if in_kernel_sum:
        for copy in road_copies:
            copy.wait()
        total = spread_out[r]
        for i in range(n_road - 1):
            total = total + road_recv[i]
        reduced[...] = total
        blk_copies = []
        for offset in range(1, n_blk):
            copy = pltpu.make_async_remote_copy(
                src_ref=reduced.at[lax.rem(b + offset, n_blk)],
                dst_ref=blk_recv.at[offset - 1],
                send_sem=blk_sems.at[0, offset - 1],
                recv_sem=blk_sems.at[1, offset - 1],
                device_id=blk_peer(offset),
                device_id_type=MESH,
            )
            copy.start()
            blk_copies.append(copy)

    for copy in halos1:
        copy.wait()
    rim_force(1)

    def finish(k, _):
        at = layer_rows(k)
        scale = time_step / mass[at, :]
        for c in range(3):
            v_out[c, at, :] = v1[c, at, :] + scale * force[c, at, :]
        return 0

    lax.fori_loop(0, layers, finish, 0)

    if in_kernel_sum:
        for copy in blk_copies:
            copy.wait()
        total = reduced[b]
        for i in range(n_blk - 1):
            total = total + blk_recv[i]
        load_out[...] = total


def on_device(
    n_blk,
    n_road,
    disp,
    veloc,
    stiff,
    mass,
    road_height,
    road_slope_x,
    road_slope_y,
    road_stiff,
    tile_list,
    pair_node,
    pair_slot,
    pair_count,
):
    _, layers, lat, lanes = disp.shape
    rows = layers * lat
    pairs = pair_node.shape[-1]
    groups = pairs // GROUP
    tiles_need = tile_list.shape[-1]
    patch_rows = road_height.shape[0] // LANES
    total_rows = patch_rows * n_road
    table_rows = tiles_need * TILE // LANES
    devices = n_blk * n_road
    in_kernel_sum = total_rows % devices == 0
    f32 = jnp.float32
    if in_kernel_sum:
        load_shape = (total_rows // devices, LANES)
    else:
        load_shape = (total_rows, LANES)
    scratch = [
        pltpu.VMEM((3, rows, lanes), f32),
        pltpu.VMEM((3, rows, lanes), f32),
        pltpu.VMEM((3, rows, lanes), f32),
        pltpu.VMEM((groups, LANES, GROUP), jnp.bfloat16),
        pltpu.VMEM((groups, LANES, GROUP), jnp.bfloat16),
        pltpu.VMEM((groups, 4, GROUP), f32),
        pltpu.VMEM((4 * n_road, patch_rows, LANES), f32),
        pltpu.VMEM((4, table_rows, LANES), f32),
        pltpu.VMEM((2, 3, rows), f32),
        pltpu.VMEM((2, 4, rows), f32),
        pltpu.VMEM((2, 3, rows), f32),
        pltpu.VMEM((2, 4, rows), f32),
        pltpu.VMEM((2, 3, layers, lanes), f32),
        pltpu.VMEM((2, 4, layers, lanes), f32),
        pltpu.VMEM((2, 3, layers, lanes), f32),
        pltpu.VMEM((2, 4, layers, lanes), f32),
        pltpu.SemaphoreType.DMA((2, 2, 4)),
        pltpu.SemaphoreType.DMA((2, 4, n_road - 1)),
    ]
    if in_kernel_sum:
        scratch += [
            pltpu.VMEM((n_road, n_blk) + load_shape, f32),
            pltpu.VMEM((n_road - 1, n_blk) + load_shape, f32),
            pltpu.VMEM((n_blk,) + load_shape, f32),
            pltpu.VMEM((n_blk - 1,) + load_shape, f32),
            pltpu.SemaphoreType.DMA((2, n_road - 1)),
            pltpu.SemaphoreType.DMA((2, n_blk - 1)),
        ]
    vmem = pl.BlockSpec(memory_space=pltpu.VMEM)
    smem = pl.BlockSpec(memory_space=pltpu.SMEM)
    velocity, load = pl.pallas_call(
        functools.partial(kernel, n_blk, n_road, lat, in_kernel_sum),
        out_shape=(
            jax.ShapeDtypeStruct((3, rows, lanes), f32),
            jax.ShapeDtypeStruct(load_shape, f32),
        ),
        in_specs=[vmem] * 8 + [smem, vmem, vmem, smem],
        out_specs=(vmem, vmem),
        scratch_shapes=scratch,
        compiler_params=pltpu.CompilerParams(collective_id=0, has_side_effects=True),
    )(
        disp.reshape(3, rows, lanes),
        veloc.reshape(3, rows, lanes),
        stiff.reshape(3, rows, lanes),
        mass.reshape(rows, lanes),
        road_height.reshape(patch_rows, LANES),
        road_slope_x.reshape(patch_rows, LANES),
        road_slope_y.reshape(patch_rows, LANES),
        road_stiff.reshape(patch_rows, LANES),
        tile_list.reshape(1, tiles_need),
        pair_node.reshape(1, pairs),
        pair_slot.reshape(1, pairs),
        pair_count.reshape(1, 1),
    )
    load = load.reshape(-1)
    if not in_kernel_sum:
        load = lax.psum_scatter(load, ("blk", "road"), scatter_dimension=0, tiled=True)
    return velocity.reshape(disp.shape), load


def solution(mesh):
    in_specs = (
        P(None, None, "road", "blk"),
        P(None, None, "road", "blk"),
        P(None, None, "road", "blk"),
        P(None, "road", "blk"),
        P("road"),
        P("road"),
        P("road"),
        P("road"),
        P("blk", "road", None),
        P("blk", "road", None),
        P("blk", "road", None),
        P("blk", "road"),
    )
    out_specs = (P(None, None, "road", "blk"), P(("blk", "road")))
    body = functools.partial(on_device, mesh.shape["blk"], mesh.shape["road"])
    return jax.shard_map(body, mesh=mesh, in_specs=in_specs, out_specs=out_specs, check_vma=False)
```

time: 839 us -> 32.7 us (0.04)
  waiting for transfers between devices: 509 us -> 0 us
  local copies, waits for them, and re-layouts: 144 us -> 2.35 us
  other arithmetic: 118 us -> 0 us
  starting transfers between devices: 29.8 us -> 0 us
  Pallas kernels: 0 us -> 28.8 us
  blocking collectives: 20.9 us -> 0 us
  between operations: 16.2 us -> 1.3 us
    unnamed x2 -> x0, waiting for transfers between devices: 361 us -> none
    ppermute x13 -> x0, waiting for transfers between devices: 148 us -> none  [the longest x4 147 us: with_halo(): lax.ppermute(lax.slice_in_dim(block, 0, width, axis=dim), axis, backward)]
    gather x8 -> x0, local copies, waits for them, and re-layouts: 129 us -> none  [the longest x4 36.5 us: gather_pairs(): picked = outer_layer[:, node_ids]]
    scatter-add x6 -> x0, other arithmetic: 93.8 us -> none  [the longest x2 47.7 us: deposit(): load_acc.at[facet_ids].add(normal_force)]
    ppermute x13 -> x0, starting transfers between devices: 29.8 us -> none  [the longest x5 13.6 us: shifted(): return lax.ppermute(block, axis, route)]
    pallas_call x0 -> x1, Pallas kernels: none -> 28.8 us  [on_device(): pl.pallas_call(functools.partial(kernel, n_blk, n_road, lat, in_kernel_su...]
    all_gather x4 -> x0, blocking collectives: 20.9 us -> none  [the longest x1 5.24 us: on_device(): lax.all_gather(road_slope_x, 'road', axis=0, tiled=True)]
  transfers between devices with their start and end apart: 14 -> 0, of which waited for: 4 -> 0; matrix products, arithmetic and copies ran while one was open for 21% -> 0% of each run, Pallas kernels for 0% -> 0%
where the time goes in v1:
time: 32.7 us; the launch traced here: 32.5 us
  Pallas kernels  28.8 us (88%)
  local copies, waits for them, and re-layouts  2.35 us (7%)
  between operations  1.3 us (4%)
    pallas_call x1, Pallas kernels, on_device(): pl.pallas_call(functools.partial(kernel, n_blk, n_road, lat, in_kernel_su...  28.8 us
    unnamed x4, local copies, waits for them, and re-layouts  2.35 us

profile of v1, /device:TPU:0, one launch (start us, length us, event | category | flops | bytes accessed | tf_op | source)
XLA Modules:
  0.0 32.5 jit_solution(5201331301110372197)
XLA Ops:
  1.3 28.8 %shard_map.131 = (f32[3,256,128]{2,1,0:T(8,128)}, f32[4,128]{1,0:T(4,128)}) custom-call(f32[3,256,128]{2,1,0:T(8,128)} %bitcast.14, f32[3,256,128]{2,1,0:T(8,128)} %bitcast.15, f32[3,256,128]{2,1,0:T(8,128)} %bitcast.16, f32[256,128]{1,0:T(8,128)} %bitcast.17, f32[32,128]{1,0:T(8,128)} %bitcast.20, f32[32,128]{1,0:T(8,128)} %bitcast.21, f32[32,128]{1,0:T(8,128)} %bitcast.22, ...), custom_call_target="tpu_custom_call" | custom-call | tf_op jit(solution)/shard_map/pallas_call | solution.py:453
  30.1 0.0 copy-start
  30.1 1.8 %copy.17 = f32[3,16,16,128]{3,2,1,0:T(8,128)} copy(f32[3,16,16,128]{3,2,1,0:T(8,128)} %bitcast.13) | data formatting | bytes 786432
  31.9 0.0 copy-done
  31.9 0.6 %copy.18 = f32[512]{0:T(512)} copy(f32[512]{0:T(512)S(1)} %bitcast.24) | data formatting | bytes 4096
Async XLA Ops:
  30.1 1.8 %copy-start = (f32[4,128]{1,0:T(4,128)S(1)}, f32[4,128]{1,0:T(4,128)}, u32[]{:S(2)}) copy-start(f32[4,128]{1,0:T(4,128)} %get-tuple-element.5) | copy-start | bytes 6148

commit v2 on v1

--- a/solution.py
+++ b/solution.py
@@ -34,20 +34,29 @@
     n_road,
     lat,
     in_kernel_sum,
-    disp,
-    veloc,
-    stiff,
-    mass,
+    disp_in,
+    veloc_in,
+    stiff_in,
+    mass_in,
     height,
     slope_x,
     slope_y,
     road_stiff,
     tiles,
-    nodes,
-    slots,
+    nodes_in,
+    slots_in,
     count,
     v_out,
     load_out,
+    disp,
+    veloc,
+    stiff,
+    mass,
+    nodes,
+    slots,
+    in_sems,
+    own_sems,
+    picked_vals,
     u1,
     v1,
     force,
@@ -120,7 +129,32 @@
             for i, (src, dst, peer) in enumerate(plan)
         ]
 
+    loads_in = [
+        pltpu.make_async_copy(src, dst, in_sems.at[i])
+        for i, (src, dst) in enumerate(
+            (
+                (disp_in, disp),
+                (stiff_in, stiff),
+                (nodes_in, nodes),
+                (slots_in, slots),
+                (mass_in, mass),
+                (veloc_in, veloc),
+            )
+        )
+    ]
+    for copy in loads_in:
+        copy.start()
+    own = (height, slope_x, slope_y, road_stiff)
+    own_copies = [
+        pltpu.make_async_copy(own[a], facet_all.at[a * n_road + r], own_sems.at[a]) for a in range(4)
+    ]
+    for copy in own_copies:
+        copy.start()
+    for copy in loads_in[:2]:
+        copy.wait()
     fill_faces(0, disp)
+    for copy in loads_in[2:4]:
+        copy.wait()
 
     def make_hot(g, _):
         at = pl.ds(pl.multiple_of(g * GROUP, GROUP), GROUP)
@@ -131,13 +165,12 @@
         facet_hot[g] = jnp.where(lane == slot_lane, 1.0, 0.0).astype(jnp.bfloat16)
         return 0
 
-    lax.fori_loop(0, groups, make_hot, 0)
+    lax.fori_loop(0, groups, make_hot, 0, unroll=2)
 
     pl.semaphore_wait(barrier, len(blk_offsets) + n_road - 1)
     halos0 = halo_copies(0)
     for copy in halos0:
         copy.start()
-    own = (height, slope_x, slope_y, road_stiff)
     facet_copies = []
     for offset in range(1, n_road):
         for a in range(4):
@@ -151,9 +184,6 @@
             )
             copy.start()
             facet_copies.append(copy)
-    for a in range(4):
-        facet_all[a * n_road + r] = own[a][...]
-
     lat_index = lax.broadcasted_iota(jnp.int32, (lat, LANES), 0)
     lane_index = lax.broadcasted_iota(jnp.int32, (lat, LANES), 1)
 
@@ -187,7 +217,7 @@
         def body(i, above):
             return tuple(inside(source, layers - 1 - i, above, False))
 
-        above = lax.fori_loop(0, layers - 1, body, nothing)
+        above = lax.fori_loop(0, layers - 1, body, nothing, unroll=3)
         inside(source, 0, above, True)
 
     def rim_force(step):
@@ -215,26 +245,42 @@
 
     live_count = count[0, 0]
 
-    def contact(source):
-        outer = [source[c, rows - lat : rows, :] for c in range(3)]
-        parts = [split_two(x) for x in outer]
-        picked_from = jnp.concatenate([p[0] for p in parts] + [p[1] for p in parts], axis=0).astype(jnp.bfloat16)
-        node_row = lax.broadcasted_iota(jnp.int32, (lat, GROUP), 0)
-        facet_row = lax.broadcasted_iota(jnp.int32, (n_rows, GROUP), 0)
-        slot_lane = lax.broadcasted_iota(jnp.int32, (1, GROUP), 1)
-
+    node_row = lax.broadcasted_iota(jnp.int32, (lat, GROUP), 0)
+    facet_row = lax.broadcasted_iota(jnp.int32, (n_rows, GROUP), 0)
+    slot_lane = lax.broadcasted_iota(jnp.int32, (1, GROUP), 1)
+
+    def split_rows(arrays):
+        parts = [split_two(x) for x in arrays]
+        return jnp.concatenate([p[0] for p in parts] + [p[1] for p in parts], axis=0).astype(jnp.bfloat16)
+
+    def group_at(g):
+        return pl.ds(pl.multiple_of(g * GROUP, GROUP), GROUP)
+
+    def look(table_rows, hot, mask, height_of):
+        found = jnp.dot(table_rows, hot, preferred_element_type=jnp.float32)
+        arrays = found.shape[0] // (2 * height_of)
+        out = []
+        for a in range(arrays):
+            both = (
+                found[a * height_of : (a + 1) * height_of]
+                + found[(arrays + a) * height_of : (arrays + a + 1) * height_of]
+            )
+            out.append(jnp.sum(jnp.where(mask, both, 0.0), axis=0, keepdims=True))
+        return out
+
+    def outer_rows(source):
+        return split_rows([source[c, rows - lat : rows, :] for c in range(3)])
+
+    def on_nodes(g):
+        return node_row == (nodes[:, group_at(g)] >> 7)
+
+    def contact(find_nodes, find_facets):
         def body(g, carry):
             pushed, loads = carry
-            at = pl.ds(pl.multiple_of(g * GROUP, GROUP), GROUP)
-            on_node = node_row == (nodes[:, at] >> 7)
-            on_facet = facet_row == (slots[:, at] >> 7)
-            found = jnp.dot(picked_from, node_hot[g], preferred_element_type=jnp.float32)
-            u = []
-            for c in range(3):
-                both = found[c * lat : (c + 1) * lat] + found[(3 + c) * lat : (4 + c) * lat]
-                u.append(jnp.sum(jnp.where(on_node, both, 0.0), axis=0, keepdims=True))
-            values = facet_vals[g]
-            h, sx, sy, ks = (values[a : a + 1, :] for a in range(4))
+            on_node = on_nodes(g)
+            on_facet = facet_row == (slots[:, group_at(g)] >> 7)
+            u = find_nodes(g, on_node)
+            h, sx, sy, ks = find_facets(g, on_facet)
             live = slot_lane + g * GROUP < live_count
             normal = jnp.where(live, ks * jnp.maximum(h + sx * u[0] + sy * u[1] - u[2], 0.0), 0.0)
             high, low = zip(*[split_two(x) for x in (-sx * normal, -sy * normal, normal)])
@@ -253,6 +299,7 @@
             groups,
             body,
             (jnp.zeros((6 * lat, LANES), jnp.float32), jnp.zeros((2 * n_rows, LANES), jnp.float32)),
+            unroll=4,
         )
         outer_force = [pushed[c * lat : (c + 1) * lat] + pushed[(3 + c) * lat : (4 + c) * lat] for c in range(3)]
         return outer_force, loads[:n_rows] + loads[n_rows:]
@@ -262,7 +309,17 @@
             force[c, rows - lat : rows, :] = force[c, rows - lat : rows, :] + outer_force[c]
 
     interior(disp)
-
+    first_outer = outer_rows(disp)
+
+    def pick_first(g, _):
+        for c, x in enumerate(look(first_outer, node_hot[g], on_nodes(g), lat)):
+            picked_vals[g, c : c + 1, :] = x
+        return 0
+
+    lax.fori_loop(0, groups, pick_first, 0, unroll=4)
+
+    for copy in own_copies + loads_in[4:]:
+        copy.wait()
     for copy in facet_copies:
         copy.wait()
     for j in range(tiles.shape[1]):
@@ -272,20 +329,18 @@
                 table[a, j * half + i : j * half + i + 1, :] = facet_all[
                     a * n_road + row // patch_rows, pl.ds(row % patch_rows, 1), :
                 ]
-    parts = [split_two(table[a]) for a in range(4)]
-    looked_from = jnp.concatenate([p[0] for p in parts] + [p[1] for p in parts], axis=0).astype(jnp.bfloat16)
-
-    def look_up(g, _):
-        at = pl.ds(pl.multiple_of(g * GROUP, GROUP), GROUP)
-        on_facet = lax.broadcasted_iota(jnp.int32, (n_rows, GROUP), 0) == (slots[:, at] >> 7)
-        found = jnp.dot(looked_from, facet_hot[g], preferred_element_type=jnp.float32)
+    looked_from = split_rows([table[a] for a in range(4)])
+
+    def first_nodes(g, on_node):
+        return [picked_vals[g, c : c + 1, :] for c in range(3)]
+
+    def first_facets(g, on_facet):
+        values = look(looked_from, facet_hot[g], on_facet, n_rows)
         for a in range(4):
-            both = found[a * n_rows : (a + 1) * n_rows] + found[(4 + a) * n_rows : (5 + a) * n_rows]
-            facet_vals[g, a : a + 1, :] = jnp.sum(jnp.where(on_facet, both, 0.0), axis=0, keepdims=True)
-        return 0
-
-    lax.fori_loop(0, groups, look_up, 0)
-    outer_force, loads0 = contact(disp)
+            facet_vals[g, a : a + 1, :] = values[a]
+        return values
+
+    outer_force, loads0 = contact(first_nodes, first_facets)
     add_outer(outer_force)
 
     for copy in halos0:
@@ -307,7 +362,11 @@
     for copy in halos1:
         copy.start()
 
-    outer_force, loads1 = contact(u1)
+    second_outer = outer_rows(u1)
+    outer_force, loads1 = contact(
+        lambda g, on_node: look(second_outer, node_hot[g], on_node, lat),
+        lambda g, on_facet: [facet_vals[g, a : a + 1, :] for a in range(4)],
+    )
     loads = loads0 + loads1
 
     def dense(shape, row_of):
@@ -423,6 +482,15 @@
         pltpu.VMEM((3, rows, lanes), f32),
         pltpu.VMEM((3, rows, lanes), f32),
         pltpu.VMEM((3, rows, lanes), f32),
+        pltpu.VMEM((rows, lanes), f32),
+        pltpu.VMEM((1, pairs), jnp.int32),
+        pltpu.VMEM((1, pairs), jnp.int32),
+        pltpu.SemaphoreType.DMA((6,)),
+        pltpu.SemaphoreType.DMA((4,)),
+        pltpu.VMEM((groups, 3, GROUP), f32),
+        pltpu.VMEM((3, rows, lanes), f32),
+        pltpu.VMEM((3, rows, lanes), f32),
+        pltpu.VMEM((3, rows, lanes), f32),
         pltpu.VMEM((groups, LANES, GROUP), jnp.bfloat16),
         pltpu.VMEM((groups, LANES, GROUP), jnp.bfloat16),
         pltpu.VMEM((groups, 4, GROUP), f32),
@@ -449,14 +517,15 @@
             pltpu.SemaphoreType.DMA((2, n_blk - 1)),
         ]
     vmem = pl.BlockSpec(memory_space=pltpu.VMEM)
+    hbm = pl.BlockSpec(memory_space=pl.ANY)
     smem = pl.BlockSpec(memory_space=pltpu.SMEM)
     velocity, load = pl.pallas_call(
         functools.partial(kernel, n_blk, n_road, lat, in_kernel_sum),
         out_shape=(
-            jax.ShapeDtypeStruct((3, rows, lanes), f32),
-            jax.ShapeDtypeStruct(load_shape, f32),
+            pltpu.VMEM((3, rows, lanes), f32),
+            pltpu.VMEM(load_shape, f32),
         ),
-        in_specs=[vmem] * 8 + [smem, vmem, vmem, smem],
+        in_specs=[hbm] * 8 + [smem, hbm, hbm, smem],
         out_specs=(vmem, vmem),
         scratch_shapes=scratch,
         compiler_params=pltpu.CompilerParams(collective_id=0, has_side_effects=True),

time: 32.7 us -> 27.6 us (0.84)
  Pallas kernels: 28.8 us -> 24.8 us
  local copies, waits for them, and re-layouts: 2.35 us -> 1.33 us
    pallas_call x1, Pallas kernels: 28.8 us -> 24.8 us  [on_device(): pl.pallas_call(functools.partial(kernel, n_blk, n_road, lat, in_kernel_su...]
    unnamed x4 -> x2, local copies, waits for them, and re-layouts: 2.35 us -> 1.33 us
where the time goes in v2:
time: 27.6 us; the launch traced here: 27.4 us
  Pallas kernels  24.8 us (90%)
  local copies, waits for them, and re-layouts  1.33 us (5%)
  between operations  1.29 us (5%)
    pallas_call x1, Pallas kernels, on_device(): pl.pallas_call(functools.partial(kernel, n_blk, n_road, lat, in_kernel_su...  24.8 us
    unnamed x2, local copies, waits for them, and re-layouts  1.33 us

profile of v2, /device:TPU:0, one launch (start us, length us, event | category | flops | bytes accessed | tf_op | source)
XLA Modules:
  0.0 27.4 jit_solution(10192054662391105475)
XLA Ops:
  1.3 24.8 %shard_map.131 = (f32[3,256,128]{2,1,0:T(8,128)S(1)}, f32[4,128]{1,0:T(4,128)S(1)}) custom-call(f32[3,256,128]{2,1,0:T(8,128)} %bitcast.15, f32[3,256,128]{2,1,0:T(8,128)} %bitcast.16, f32[3,256,128]{2,1,0:T(8,128)} %bitcast.17, f32[256,128]{1,0:T(8,128)} %bitcast.18, f32[32,128]{1,0:T(8,128)} %bitcast.21, f32[32,128]{1,0:T(8,128)} %bitcast.22, ...), custom_call_target="tpu_custom_call" | custom-call | tf_op jit(solution)/shard_map/pallas_call | solution.py:522
  26.1 0.7 %copy.16 = f32[3,16,16,128]{3,2,1,0:T(8,128)} copy(f32[3,16,16,128]{3,2,1,0:T(8,128)S(1)} %bitcast.13) | data formatting | bytes 786432
  26.9 0.6 %copy.17 = f32[512]{0:T(512)} copy(f32[512]{0:T(512)S(1)} %bitcast.14) | data formatting | bytes 4096

commit v3 on v2

--- a/solution.py
+++ b/solution.py
@@ -57,6 +57,7 @@
     in_sems,
     own_sems,
     picked_vals,
+    normals,
     u1,
     v1,
     force,
@@ -274,35 +275,33 @@
     def on_nodes(g):
         return node_row == (nodes[:, group_at(g)] >> 7)
 
-    def contact(find_nodes, find_facets):
-        def body(g, carry):
-            pushed, loads = carry
-            on_node = on_nodes(g)
-            on_facet = facet_row == (slots[:, group_at(g)] >> 7)
-            u = find_nodes(g, on_node)
-            h, sx, sy, ks = find_facets(g, on_facet)
-            live = slot_lane + g * GROUP < live_count
-            normal = jnp.where(live, ks * jnp.maximum(h + sx * u[0] + sy * u[1] - u[2], 0.0), 0.0)
-            high, low = zip(*[split_two(x) for x in (-sx * normal, -sy * normal, normal)])
-            spread = jnp.concatenate([jnp.where(on_node, x, 0.0) for x in high + low], axis=0)
-            pushed = pushed + lax.dot_general(
-                spread.astype(jnp.bfloat16), node_hot[g], NT, preferred_element_type=jnp.float32
-            )
-            heaped = jnp.concatenate([jnp.where(on_facet, x, 0.0) for x in (high[2], low[2])], axis=0)
-            loads = loads + lax.dot_general(
-                heaped.astype(jnp.bfloat16), facet_hot[g], NT, preferred_element_type=jnp.float32
-            )
-            return pushed, loads
-
-        pushed, loads = lax.fori_loop(
-            0,
-            groups,
-            body,
-            (jnp.zeros((6 * lat, LANES), jnp.float32), jnp.zeros((2 * n_rows, LANES), jnp.float32)),
-            unroll=4,
-        )
-        outer_force = [pushed[c * lat : (c + 1) * lat] + pushed[(3 + c) * lat : (4 + c) * lat] for c in range(3)]
-        return outer_force, loads[:n_rows] + loads[n_rows:]
+    def press(g, u, h, sx, sy, ks):
+        live = slot_lane + g * GROUP < live_count
+        return jnp.where(live, ks * jnp.maximum(h + sx * u[0] + sy * u[1] - u[2], 0.0), 0.0)
+
+    def gather_force(g, on_node, sx, sy, normal, pushed):
+        high, low = zip(*[split_two(x) for x in (-sx * normal, -sy * normal, normal)])
+        spread = jnp.concatenate([jnp.where(on_node, x, 0.0) for x in high + low], axis=0)
+        return pushed + lax.dot_general(
+            spread.astype(jnp.bfloat16), node_hot[g], NT, preferred_element_type=jnp.float32
+        )
+
+    def gather_load(g, on_facet, normal, loads):
+        heaped = jnp.concatenate([jnp.where(on_facet, x, 0.0) for x in split_two(normal)], axis=0)
+        return loads + lax.dot_general(
+            heaped.astype(jnp.bfloat16), facet_hot[g], NT, preferred_element_type=jnp.float32
+        )
+
+    def on_facets(g):
+        return facet_row == (slots[:, group_at(g)] >> 7)
+
+    def stored_facet(g, a):
+        return facet_vals[g, a : a + 1, :]
+
+    no_push = jnp.zeros((6 * lat, LANES), jnp.float32)
+
+    def outer_sum(pushed):
+        return [pushed[c * lat : (c + 1) * lat] + pushed[(3 + c) * lat : (4 + c) * lat] for c in range(3)]
 
     def add_outer(outer_force):
         for c in range(3):
@@ -320,6 +319,21 @@
 
     for copy in own_copies + loads_in[4:]:
         copy.wait()
+    for copy in halos0:
+        copy.wait()
+    rim_force(0)
+
+    def advance(k, _):
+        at = layer_rows(k)
+        scale = time_step / mass[at, :]
+        for c in range(3):
+            v = veloc[c, at, :] + scale * force[c, at, :]
+            v1[c, at, :] = v
+            u1[c, at, :] = disp[c, at, :] + time_step * v
+        return 0
+
+    lax.fori_loop(0, layers - 1, advance, 0)
+
     for copy in facet_copies:
         copy.wait()
     for j in range(tiles.shape[1]):
@@ -331,43 +345,30 @@
                 ]
     looked_from = split_rows([table[a] for a in range(4)])
 
-    def first_nodes(g, on_node):
-        return [picked_vals[g, c : c + 1, :] for c in range(3)]
-
-    def first_facets(g, on_facet):
-        values = look(looked_from, facet_hot[g], on_facet, n_rows)
+    def first_contact(g, pushed):
+        values = look(looked_from, facet_hot[g], on_facets(g), n_rows)
         for a in range(4):
             facet_vals[g, a : a + 1, :] = values[a]
-        return values
-
-    outer_force, loads0 = contact(first_nodes, first_facets)
-    add_outer(outer_force)
-
-    for copy in halos0:
-        copy.wait()
-    rim_force(0)
-
-    def advance(k, _):
-        at = layer_rows(k)
-        scale = time_step / mass[at, :]
-        for c in range(3):
-            v = veloc[c, at, :] + scale * force[c, at, :]
-            v1[c, at, :] = v
-            u1[c, at, :] = disp[c, at, :] + time_step * v
-        return 0
-
-    lax.fori_loop(0, layers, advance, 0)
-    fill_faces(1, u1)
-    halos1 = halo_copies(1)
-    for copy in halos1:
-        copy.start()
+        h, sx, sy, ks = values
+        normal = press(g, [picked_vals[g, c : c + 1, :] for c in range(3)], h, sx, sy, ks)
+        normals[g, 0:1, :] = normal
+        return gather_force(g, on_nodes(g), sx, sy, normal, pushed)
+
+    add_outer(outer_sum(lax.fori_loop(0, groups, first_contact, no_push, unroll=4)))
+    advance(layers - 1, 0)
 
     second_outer = outer_rows(u1)
-    outer_force, loads1 = contact(
-        lambda g, on_node: look(second_outer, node_hot[g], on_node, lat),
-        lambda g, on_facet: [facet_vals[g, a : a + 1, :] for a in range(4)],
+
+    def second_press(g, loads):
+        u = look(second_outer, node_hot[g], on_nodes(g), lat)
+        normal = press(g, u, *[stored_facet(g, a) for a in range(4)])
+        normals[g, 1:2, :] = normal
+        return gather_load(g, on_facets(g), normal + normals[g, 0:1, :], loads)
+
+    loads = lax.fori_loop(
+        0, groups, second_press, jnp.zeros((2 * n_rows, LANES), jnp.float32), unroll=4
     )
-    loads = loads0 + loads1
+    loads = loads[:n_rows] + loads[n_rows:]
 
     def dense(shape, row_of):
         row = row_of(shape)
@@ -402,8 +403,11 @@
     else:
         load_out[...] = dense(load_out.shape, lambda s: lax.broadcasted_iota(jnp.int32, s, 0))
 
+    fill_faces(1, u1)
+    halos1 = halo_copies(1)
+    for copy in halos1:
+        copy.start()
     interior(u1)
-    add_outer(outer_force)
 
     if in_kernel_sum:
         for copy in road_copies:
@@ -425,6 +429,12 @@
             copy.start()
             blk_copies.append(copy)
 
+    def second_contact(g, pushed):
+        return gather_force(
+            g, on_nodes(g), stored_facet(g, 1), stored_facet(g, 2), normals[g, 1:2, :], pushed
+        )
+
+    add_outer(outer_sum(lax.fori_loop(0, groups, second_contact, no_push, unroll=4)))
     for copy in halos1:
         copy.wait()
     rim_force(1)
@@ -488,6 +498,7 @@
         pltpu.SemaphoreType.DMA((6,)),
         pltpu.SemaphoreType.DMA((4,)),
         pltpu.VMEM((groups, 3, GROUP), f32),
+        pltpu.VMEM((groups, 2, GROUP), f32),
         pltpu.VMEM((3, rows, lanes), f32),
         pltpu.VMEM((3, rows, lanes), f32),
         pltpu.VMEM((3, rows, lanes), f32),

time: 27.6 us -> 26.1 us (0.946)
  Pallas kernels: 24.8 us -> 23.3 us
    pallas_call x1, Pallas kernels: 24.8 us -> 23.3 us  [on_device(): pl.pallas_call(functools.partial(kernel, n_blk, n_road, lat, in_kernel_su...]
where the time goes in v3:
time: 26.1 us; the launch traced here: 25.9 us
  Pallas kernels  23.3 us (89%)
  local copies, waits for them, and re-layouts  1.33 us (5%)
  between operations  1.29 us (5%)
    pallas_call x1, Pallas kernels, on_device(): pl.pallas_call(functools.partial(kernel, n_blk, n_road, lat, in_kernel_su...  23.3 us
    unnamed x2, local copies, waits for them, and re-layouts  1.33 us

profile of v3, /device:TPU:0, one launch (start us, length us, event | category | flops | bytes accessed | tf_op | source)
XLA Modules:
  0.0 25.9 jit_solution(11738864257894957561)
XLA Ops:
  1.3 23.3 %shard_map.131 = (f32[3,256,128]{2,1,0:T(8,128)S(1)}, f32[4,128]{1,0:T(4,128)S(1)}) custom-call(f32[3,256,128]{2,1,0:T(8,128)} %bitcast.15, f32[3,256,128]{2,1,0:T(8,128)} %bitcast.16, f32[3,256,128]{2,1,0:T(8,128)} %bitcast.17, f32[256,128]{1,0:T(8,128)} %bitcast.18, f32[32,128]{1,0:T(8,128)} %bitcast.21, f32[32,128]{1,0:T(8,128)} %bitcast.22, ...), custom_call_target="tpu_custom_call" | custom-call | tf_op jit(solution)/shard_map/pallas_call | solution.py:533
  24.6 0.7 %copy.16 = f32[3,16,16,128]{3,2,1,0:T(8,128)} copy(f32[3,16,16,128]{3,2,1,0:T(8,128)S(1)} %bitcast.13) | data formatting | bytes 786432
  25.3 0.6 %copy.17 = f32[512]{0:T(512)} copy(f32[512]{0:T(512)S(1)} %bitcast.14) | data formatting | bytes 4096
